TPU v7x, 32 devices: a whole 2x2x4 slice. The times are simulated.
32 devices in a mesh: comp: 2 (over y), gx: 4 (over x, core), gy: 4 (over z).
Axes of the slice: x: 2, y: 2, z: 4, core: 2. Of those that a mesh axis runs over, the one named last changes fastest.
Arguments:
- state: float32 [2, 30, 128, 1024], P('comp', None, 'gx', 'gy'), may hold values from -6 to 6
- conduct: float32 [2, 30, 128, 1024], P('comp', None, 'gx', 'gy'), may hold values from 0.3 to 3
- storage: float32 [2], P('comp'), may hold values from 0.05 to 0.5
- surface_source: float32 [2, 128, 1024], P('comp', 'gx', 'gy'), may hold values from -6 to 6
- plant_type: int32 [2, 128, 1024], P('comp', 'gx', 'gy'), may hold values from 0 to 15
- plant_table: float32 [16, 2], replicated, may hold values from 0.3 to 3
- layer_weights: float32 [2, 16, 6], replicated, may hold values from 0.05 to 1
- remap_rows: int32 [2, 128], P('comp', 'gx'), may hold values from 0 to 31
- remap_weights: float32 [2, 1024, 128], P('comp', 'gy'), may hold values from 0 to 1
Outputs:
- new_state: float32 [2, 30, 128, 1024], P('comp', None, 'gx', 'gy')
- exchange_flux: float32 [2, 128, 1024], P('comp', 'gx', 'gy')
All inputs are finite; a program needn't handle non-finite values.
Results may differ from a plain program's by a relative error of at most 0.0003.
Values sent between devices are 32-bit elements; how exact they have to be, the bound alone decides.
No kernel may reach another device: no remote copies, remote signals or barrier semaphores. Data moves between devices by JAX's collectives and lax.ppermute only.
A program may use at most 64 MiB of HBM per device.

v0:
```python
import jax
import jax.numpy as jnp
from jax import lax
from jax.sharding import PartitionSpec as P

NS = 6
PATCH = 128
PLANTS = 16
ITERS = 3


def from_partner(value, axis, distance):
    mask = 2**distance
    pairs = [(source, source ^ mask) for source in range(lax.axis_size(axis))]
    return lax.ppermute(value, axis, pairs)


def extended(block, sides, width):
    for axis, dim in sides:
        count = lax.axis_size(axis)
        forward = [(i, i + 1) for i in range(count - 1)]
        backward = [(target, source) for source, target in forward]
        low = lax.ppermute(
            lax.slice_in_dim(block, block.shape[dim] - width, None, axis=dim), axis, forward
        )
        high = lax.ppermute(lax.slice_in_dim(block, 0, width, axis=dim), axis, backward)
        block = jnp.concatenate([low, block, high], axis=dim)
    return block


def apply_padded(vp, kp):
    v = vp[1:-1, 1:-1, 1:-1]
    kc = kp[1:-1, 1:-1, 1:-1]
    total = jnp.zeros_like(v)
    moves = [(2, 1, 1), (0, 1, 1), (1, 2, 1), (1, 0, 1), (1, 1, 2), (1, 1, 0)]
    for a, b, e in moves:
        vn = vp[a : a + v.shape[0], b : b + v.shape[1], e : e + v.shape[2]]
        kn = kp[a : a + v.shape[0], b : b + v.shape[1], e : e + v.shape[2]]
        total = total + 0.5 * (kc + kn) * (v - vn)
    return total


def pad_levels(field):
    return jnp.pad(field, ((1, 1), (0, 0), (0, 0)))


def least_squares(hmat, beta):
    gram = jnp.sum(hmat[:, :, None] * hmat[:, None, :], axis=0)
    target_vector = beta * hmat[0, :]
    factor = jnp.linalg.cholesky(gram)
    return jax.scipy.linalg.cho_solve((factor, True), target_vector)


def one_hot_types(kinds):
    return (kinds[None, :, :] == jnp.arange(PLANTS)[:, None, None]).astype(jnp.float32)


def forcing_for(layers, rows, weights, kinds, profile):
    hp = lax.Precision.HIGHEST
    picked = jnp.take(layers, rows, axis=1)
    width = layers.shape[2]
    blocks = picked.reshape(layers.shape[0], layers.shape[1], width // PATCH, PATCH)
    wblk = weights.reshape(width // PATCH, PATCH, PATCH)
    remapped = jnp.einsum("lxbk,bjk->lxbj", blocks, wblk, precision=hp).reshape(layers.shape)
    prof = jnp.einsum("pl,pxy->lxy", profile, one_hot_types(kinds), precision=hp)
    return jnp.sum(prof * remapped, axis=0)


def body(
    state,
    conduct,
    storage,
    surface_source,
    plant_type,
    plant_table,
    layer_weights,
    remap_rows,
    remap_weights,
):
    hp = lax.Precision.HIGHEST
    comp_index = lax.axis_index("comp")
    field = state[0]
    levels = field.shape[0]
    keff = conduct[0] * (1.0 + 0.5 * jnp.tanh(field))
    kinds = plant_type[0]
    own_table = jnp.where(comp_index == 0, layer_weights[0], layer_weights[1])
    other_table = jnp.where(comp_index == 0, layer_weights[1], layer_weights[0])
    layers = field[:NS]
    partner_layers = from_partner(layers, "comp", 0)
    other_force = forcing_for(partner_layers, remap_rows[0], remap_weights[0], kinds, other_table)
    selector = one_hot_types(kinds)
    own_prof = jnp.einsum("pl,pxy->lxy", own_table, selector, precision=hp)
    own_force = jnp.sum(own_prof * layers, axis=0)
    atmospheric_forcing = jnp.where(comp_index == 0, own_force, other_force)
    soil_force = jnp.where(comp_index == 0, other_force, own_force)
    params = jnp.einsum("pq,pxy->qxy", plant_table, selector, precision=hp)
    flux = params[0] * (params[1] * soil_force - atmospheric_forcing)
    sign = 1.0 - 2.0 * comp_index.astype(jnp.float32)
    top = sign * flux[None] * own_prof
    source = jnp.concatenate([top, jnp.zeros((levels - NS,) + flux.shape, jnp.float32)], axis=0)
    source = source.at[0].add(surface_source[0])
    diagonal_shift = storage[0]
    depth = 1
    stacked = jnp.stack([field, keff])
    padded = extended(stacked, (("gx", 2), ("gy", 3)), depth)
    kext = padded[1]

    def apply_extended_operator(vector):
        return apply_padded(pad_levels(vector), pad_levels(kext))

    rhs_rim = 0
    rhs = source - apply_extended_operator(padded[0])
    beta = jnp.sqrt(lax.psum(jnp.sum(rhs * rhs), ("gx", "gy")))
    basis = [rhs / beta]
    rims = [rhs_rim]
    hmat = jnp.zeros((ITERS + 1, ITERS), jnp.float32)
    for j in range(ITERS):
        operate_vector = basis[j]
        padded_vector = extended(operate_vector, (("gx", 1), ("gy", 2)), 1)
        krylov_vector = diagonal_shift * operate_vector + apply_extended_operator(padded_vector)
        near = [basis[i] for i in range(j + 1)]
        interior_vector = krylov_vector
        partials = jnp.stack([jnp.sum(interior_vector * near[i]) for i in range(j + 1)])
        heights, squared = lax.psum(
            (partials, jnp.sum(interior_vector * interior_vector)), ("gx", "gy")
        )
        for i in range(j + 1):
            krylov_vector = krylov_vector - heights[i] * near[i]
            hmat = hmat.at[i, j].set(heights[i])
        nrm = jnp.sqrt(squared - jnp.sum(heights * heights))
        hmat = hmat.at[j + 1, j].set(nrm)
        if j + 1 < ITERS:
            basis.append(krylov_vector / nrm)
            rims.append(0)
    coef = least_squares(hmat, beta)
    update = field
    for j in range(ITERS):
        update = update + coef[j] * basis[j]
    return (update[None], flux[None])


def solution(mesh):
    in_specs = (
        P("comp", None, "gx", "gy"),
        P("comp", None, "gx", "gy"),
        P("comp"),
        P("comp", "gx", "gy"),
        P("comp", "gx", "gy"),
        P(),
        P(),
        P("comp", "gx"),
        P("comp", "gy", None),
    )
    out_specs = (P("comp", None, "gx", "gy"), P("comp", "gx", "gy"))
    return jax.shard_map(body, mesh=mesh, in_specs=in_specs, out_specs=out_specs, check_vma=False)
```

profile of v0, /device:TPU:0, one launch (start us, length us, event | category | flops | bytes accessed | tf_op | source)
XLA Modules:
  0.0 289.8 jit_solution(18306534450903827338)
XLA Ops:
  2.5 3.1 %collective-permute-start = (f32[6,32,256]{2,0,1:T(8,128)}, f32[6,32,256]{2,0,1:T(8,128)}, u32[]{:S(2)}, u32[]{:S(2)}) collective-permute-start(f32[6,32,256]{2,0,1:T(8,128)} %bitcast.108), channel_id=1, source_target_pairs={{0,16},{16,0},{1,17},{17,1},{2,18},{18,2},{3,19},{19,3},{4,20},{20... | collective-permute-start | bytes 589832 | tf_op jit(solution)/shard_map/ppermute | solution.py:15
  17.1 4.1 %collective-permute-start.3 = (f32[2,30,34,1]{2,0,3,1:T(2,128)S(1)}, f32[2,30,34,1]{2,0,3,1:T(2,128)}, u32[]{:S(2)}, u32[]{:S(2)}) collective-permute-start(f32[2,30,34,1]{2,0,3,1:T(2,128)S(1)} %copy.131), channel_id=1, source_target_pairs={{0,1},{1,2},{2,3},{4,5},{5,6},{6,7},{8,9},{9,10},{10,11},{12,13},{... | collective-permute-start | bytes 24488 | tf_op jit(solution)/shard_map/ppermute | solution.py:23
  28.4 2.3 copy.134
  30.7 3.2 %pad_maximum_fusion = f32[2,30,34,258]{3,2,1,0:T(8,128)S(1)} fusion(f32[2,30,34,1]{3,2,1,0:T(8,128)} %copy.134, f32[2,30,1,256]{3,2,1,0:T(1,128)S(1)} %collective-permute-done.2, f32[1,30,32,256]{3,2,1,0:T(8,128)S(1)} %add_multiply_fusion, f32[1,30,32,256]{3,2,1,0:T(8,128)S(1)} %copy-done.2, f32[2,30,1,256]{3,2,1,0:T(1,128)S(1)} %collective-permute-done.1, ...), kind=kLoop, calls=%fused_computation.1 | loop fusion | flops 2631600 | bytes 4210560 | tf_op jit(solution)/shard_map/concatenate | solution.py:27
  39.7 5.6 %multiply_reduce_fusion.9 = (f32[]{:T(128)}, f32[30,32,256]{2,1,0:T(8,128)S(1)}, f32[30,32,256]{2,1,0:T(8,128)}, f32[30,32,256]{2,1,0:T(8,128)}, f32[30,32,256]{...) fusion(f32[30,32,256]{2,1,0:T(8,128)S(1)} %fusion.80, ...), kind=kLoop, calls=%fused_computation.156 | loop fusion | flops 7864319 | bytes 21381124 | tf_op jit(solution)/shard_map/reduce_sum | solution.py:113
  45.2 34.1 %psum.49 = f32[]{:T(128)} all-reduce(f32[]{:T(128)} %get-tuple-element.149), channel_id=1, replica_groups=mesh['comp'=2,'gx'=4,'gy'=4] {'gx','gy'}, use_global_device_ids=true, to_apply=%region_3.4 | all-reduce | flops 1 | bytes 8 | tf_op jit(solution)/shard_map/psum | solution.py:113
  82.9 4.0 %collective-permute-done.6 = f32[30,1,256]{2,1,0:T(1,128)S(1)} collective-permute-done((f32[30,1,256]{2,1,0:T(1,128)S(1)}, f32[30,1,256]{2,1,0:T(1,128)S(1)}, u32[]{:S(2)}, u32[]{:S(2)}) %collective-permute-start.6) | collective-permute-done | bytes 30752 | tf_op jit(solution)/shard_map/ppermute | solution.py:26
  87.6 2.4 collective-permute-start.7
  97.1 2.4 select_maximum_fusion.8
  99.6 5.0 %multiply_reduce_fusion.8 = (f32[]{:T(128)}, f32[]{:T(128)}, f32[30,32,256]{2,1,0:T(8,128)}) fusion(f32[30,32,256]{2,1,0:T(8,128)S(1)} %broadcast_divide_fusion, f32[30,32,256]{2,1,0:T(8,128)} %get-tuple-element.156, f32[30,1,256]{2,1,0:T(1,128)S(1)} %collective-permute-done.6, f32[30,1,256]{2,1,0:T(1,128)S(1)} %collective-permute-done.5, ...), kind=kLoop, calls=%fused_computation.155 | loop fusion | flops 7618558 | bytes 9900012 | tf_op jit(solution)/shard_map/reduce_sum | solution.py:123
  104.6 30.7 %all-reduce.9 = (f32[]{:T(128)}, f32[1]{0:T(128)}) all-reduce(f32[]{:T(128)} %get-tuple-element.140, f32[1]{0:T(128)} %bitcast.21), channel_id=1, replica_groups=mesh['comp'=2,'gx'=4,'gy'=4] {'gx','gy'}, use_global_device_ids=true, to_apply=%region_7.8 | all-reduce | flops 2 | bytes 16 | tf_op jit(solution)/shard_map/psum | solution.py:124
  140.7 3.0 %collective-permute-start.9 = (f32[30,1,256]{2,1,0:T(1,128)S(1)}, f32[30,1,256]{2,1,0:T(1,128)S(1)}, u32[]{:S(2)}, u32[]{:S(2)}) collective-permute-start(f32[30,1,256]{2,1,0:T(1,128)S(1)} %get-tuple-element.173), channel_id=1, source_target_pairs={{0,4},{4,8},{8,12},{1,5},{5,9},{9,13},{2,6},{6,10},{10,14},{3,7},{... | collective-permute-start | bytes 92168 | tf_op jit(solution)/shard_map/ppermute | solution.py:23
  147.4 3.8 %collective-permute-start.11 = (f32[30,34,1]{1,2,0:T(1,128)S(1)}, f32[30,34,1]{1,2,0:T(1,128)S(1)}, u32[]{:S(2)}, u32[]{:S(2)}) collective-permute-start(f32[30,34,1]{1,2,0:T(1,128)S(1)} %copy.141), channel_id=1, source_target_pairs={{0,1},{1,2},{2,3},{4,5},{5,6},{6,7},{8,9},{9,10},{10,11},{12,13},{... | collective-permute-start | bytes 12248 | tf_op jit(solution)/shard_map/ppermute | solution.py:23
  155.7 2.5 collective-permute-done.12
  159.3 2.4 select_maximum_fusion.4
  161.8 4.9 %multiply_reduce_fusion.6 = (f32[]{:T(128)}, f32[]{:T(128)}, f32[]{:T(128)}, f32[30,32,256]{2,1,0:T(8,128)}) fusion(f32[30,32,256]{2,1,0:T(8,128)S(1)} %subtract_divide_fusion.1, f32[30,32,256]{2,1,0:T(8,128)} %get-tuple-element.156, f32[30,1,256]{2,1,0:T(1,128)S(1)} %collective-permute-done.10, f32[30,1,256]{2,1,0:T(1,128)S(1)} %collective-permute-done.9, ...), kind=kLoop, calls=%fused_computation.152 | loop fusion | flops 8355837 | bytes 10883060 | tf_op jit(solution)/shard_map/reduce_sum | solution.py:123
  168.1 30.8 %all-reduce.8 = (f32[]{:T(128)}, f32[2]{0:T(128)S(1)}) all-reduce(f32[]{:T(128)} %get-tuple-element.137, f32[2]{0:T(128)S(1)} %pad_maximum_fusion.31), channel_id=1, replica_groups=mesh['comp'=2,'gx'=4,'gy'=4] {'gx','gy'}, use_global_device_ids=true, to_apply=%region_12.13 | all-reduce | flops 3 | bytes 24 | tf_op jit(solution)/shard_map/psum | solution.py:124
  201.5 2.7 subtract_divide_fusion
  206.9 6.1 %collective-permute-done.14 = f32[30,1,256]{2,1,0:T(1,128)S(1)} collective-permute-done((f32[30,1,256]{2,1,0:T(1,128)S(1)}, f32[30,1,256]{2,1,0:T(1,128)S(1)}, u32[]{:S(2)}, u32[]{:S(2)}) %collective-permute-start.14) | collective-permute-done | bytes 30752 | tf_op jit(solution)/shard_map/ppermute | solution.py:26
  215.8 4.0 %collective-permute-start.15 = (f32[30,34,1]{1,2,0:T(1,128)S(1)}, f32[30,34,1]{1,2,0:T(1,128)S(1)}, u32[]{:S(2)}, u32[]{:S(2)}) collective-permute-start(f32[30,34,1]{1,2,0:T(1,128)S(1)} %copy.147), channel_id=1, source_target_pairs={{0,1},{1,2},{2,3},{4,5},{5,6},{6,7},{8,9},{9,10},{10,11},{12,13},{... | collective-permute-start | bytes 12248 | tf_op jit(solution)/shard_map/ppermute | solution.py:23
  231.6 2.4 select_maximum_fusion
  234.0 6.0 %multiply_reduce_fusion = (f32[]{:T(128)}, f32[]{:T(128)}, f32[]{:T(128)}, f32[]{:T(128)}) fusion(f32[30,32,256]{2,1,0:T(8,128)} %copy-done.4, f32[30,32,256]{2,1,0:T(8,128)S(1)} %subtract_divide_fusion.1, f32[30,32,256]{2,1,0:T(8,128)} %get-tuple-element.156, f32[30,1,256]{2,1,0:T(1,128)S(1)} %collective-permute-done.14, ...), kind=kLoop, calls=%fused_computation.145 | loop fusion | flops 8847356 | bytes 10883064 | tf_op jit(solution)/shard_map/reduce_sum | solution.py:125
  242.0 32.9 %all-reduce.7 = (f32[3]{0:T(128)S(1)}, f32[]{:T(128)}) all-reduce(f32[3]{0:T(128)S(1)} %pad_maximum_fusion.32, f32[]{:T(128)} %get-tuple-element.132), channel_id=1, replica_groups=mesh['comp'=2,'gx'=4,'gy'=4] {'gx','gy'}, use_global_device_ids=true, to_apply=%region_18.19 | all-reduce | flops 4 | bytes 32 | tf_op jit(solution)/shard_map/psum | solution.py:124
  285.4 4.4 %fusion.74 = f32[1,30,32,256]{3,2,1,0:T(8,128)} fusion(f32[1,30,32,256]{3,2,1,0:T(8,128)S(1)} %copy-done.3, f32[30,32,256]{2,1,0:T(8,128)} %copy-done.4, f32[30,32,256]{2,1,0:T(8,128)S(1)} %subtract_divide_fusion.1, f32[]{:T(128)} %bitcast.55, f32[]{:T(128)} %bitcast.54, f32[]{:T(128)} %bitcast.53, f32[30,32,256]{2,1,0:T(8,128)S(1)} %get-tuple-element.150, ...), kind=kLoop, calls=%fused_computation.144 | loop fusion | flops 1720320 | bytes 4915216 | tf_op jit(solution)/shard_map/broadcast_in_dim | solution.py:139
  (163 shorter events, 77.8 us)
Async XLA Ops:
  0.6 36.8 %copy-start = (f32[1,256,128]{2,1,0:T(8,128)S(1)}, f32[1,256,128]{2,1,0:T(8,128)}, u32[]{:S(2)}) copy-start(f32[1,256,128]{2,1,0:T(8,128)} %param.37) | copy-start | bytes 393220
  2.5 7.6 %copy-start.24 = (s32[1,32]{1,0:T(1,128)S(1)}, s32[1,32]{1,0:T(1,128)}, u32[]{:S(2)}) copy-start(s32[1,32]{1,0:T(1,128)} %param.36) | copy-start | bytes 388
  2.5 8.2 %copy-start.18 = (s32[1,32,256]{2,1,0:T(8,128)S(1)}, s32[1,32,256]{2,1,0:T(8,128)}, u32[]{:S(2)}) copy-start(s32[1,32,256]{2,1,0:T(8,128)} %param.33) | copy-start | bytes 98308
  2.5 8.2 %copy-start.23 = (f32[16,2]{0,1:T(2,128)S(1)}, f32[16,2]{0,1:T(2,128)}, u32[]{:S(2)}) copy-start(f32[16,2]{0,1:T(2,128)} %param.34) | copy-start | bytes 388
  2.5 32.9 %collective-permute-start = (f32[6,32,256]{2,0,1:T(8,128)}, f32[6,32,256]{2,0,1:T(8,128)}, u32[]{:S(2)}, u32[]{:S(2)}) collective-permute-start(f32[6,32,256]{2,0,1:T(8,128)} %bitcast.108), channel_id=1, source_target_pairs={{0,16},{16,0},{1,17},{17,1},{2,18},{18,2},{3,19},{19,3},{4,20},{20... | collective-permute-start | bytes 589832 | tf_op jit(solution)/shard_map/ppermute | solution.py:15
  7.4 6.0 %collective-permute-start.1 = (f32[2,30,1,256]{3,2,1,0:T(1,128)S(1)}, f32[2,30,1,256]{3,2,1,0:T(1,128)S(1)}, u32[]{:S(2)}, u32[]{:S(2)}) collective-permute-start(f32[2,30,1,256]{3,2,1,0:T(1,128)S(1)} %get-tuple-element.163), channel_id=1, source_target_pairs={{0,4},{4,8},{8,12},{1,5},{5,9},{9,13},{2,6},{6,10},{10,14},{3,7},{... | collective-permute-start | bytes 184328 | tf_op jit(solution)/shard_map/ppermute | solution.py:23
  8.8 4.7 %collective-permute-start.2 = (f32[2,30,1,256]{3,2,1,0:T(1,128)S(1)}, f32[2,30,1,256]{3,2,1,0:T(1,128)S(1)}, u32[]{:S(2)}, u32[]{:S(2)}) collective-permute-start(f32[2,30,1,256]{3,2,1,0:T(1,128)S(1)} %get-tuple-element.164), channel_id=1, source_target_pairs={{4,0},{8,4},{12,8},{5,1},{9,5},{13,9},{6,2},{10,6},{14,10},{7,3},{... | collective-permute-start | bytes 184328 | tf_op jit(solution)/shard_map/ppermute | solution.py:26
  17.1 7.8 %collective-permute-start.3 = (f32[2,30,34,1]{2,0,3,1:T(2,128)S(1)}, f32[2,30,34,1]{2,0,3,1:T(2,128)}, u32[]{:S(2)}, u32[]{:S(2)}) collective-permute-start(f32[2,30,34,1]{2,0,3,1:T(2,128)S(1)} %copy.131), channel_id=1, source_target_pairs={{0,1},{1,2},{2,3},{4,5},{5,6},{6,7},{8,9},{9,10},{10,11},{12,13},{... | collective-permute-start | bytes 24488 | tf_op jit(solution)/shard_map/ppermute | solution.py:23
  22.3 6.1 %collective-permute-start.4 = (f32[2,30,34,1]{2,0,3,1:T(2,128)}, f32[2,30,34,1]{2,0,3,1:T(2,128)}, u32[]{:S(2)}, u32[]{:S(2)}) collective-permute-start(f32[2,30,34,1]{2,0,3,1:T(2,128)} %copy.132), channel_id=1, source_target_pairs={{1,0},{2,1},{3,2},{5,4},{6,5},{7,6},{9,8},{10,9},{11,10},{13,12},{... | collective-permute-start | bytes 24488 | tf_op jit(solution)/shard_map/ppermute | solution.py:26
  80.3 2.6 collective-permute-start.5
  81.6 5.3 %collective-permute-start.6 = (f32[30,1,256]{2,1,0:T(1,128)S(1)}, f32[30,1,256]{2,1,0:T(1,128)S(1)}, u32[]{:S(2)}, u32[]{:S(2)}) collective-permute-start(f32[30,1,256]{2,1,0:T(1,128)S(1)} %get-tuple-element.176), channel_id=1, source_target_pairs={{4,0},{8,4},{12,8},{5,1},{9,5},{13,9},{6,2},{10,6},{14,10},{7,3},{... | collective-permute-start | bytes 92168 | tf_op jit(solution)/shard_map/ppermute | solution.py:26
  87.6 4.9 %collective-permute-start.7 = (f32[30,34,1]{1,2,0:T(1,128)S(1)}, f32[30,34,1]{1,2,0:T(1,128)S(1)}, u32[]{:S(2)}, u32[]{:S(2)}) collective-permute-start(f32[30,34,1]{1,2,0:T(1,128)S(1)} %copy.135), channel_id=1, source_target_pairs={{0,1},{1,2},{2,3},{4,5},{5,6},{6,7},{8,9},{9,10},{10,11},{12,13},{... | collective-permute-start | bytes 12248 | tf_op jit(solution)/shard_map/ppermute | solution.py:23
  90.3 5.6 %collective-permute-start.8 = (f32[30,34,1]{1,2,0:T(1,128)S(1)}, f32[30,34,1]{1,2,0:T(1,128)S(1)}, u32[]{:S(2)}, u32[]{:S(2)}) collective-permute-start(f32[30,34,1]{1,2,0:T(1,128)S(1)} %copy.136), channel_id=1, source_target_pairs={{1,0},{2,1},{3,2},{5,4},{6,5},{7,6},{9,8},{10,9},{11,10},{13,12},{... | collective-permute-start | bytes 12248 | tf_op jit(solution)/shard_map/ppermute | solution.py:26
  104.6 39.2 %copy-start.25 = (s32[2]{0:T(128)S(1)}, s32[2]{0:T(128)}, u32[]{:S(2)}) copy-start(s32[2]{0:T(128)} %constant.341.clone.1) | copy-start | bytes 28
  139.4 5.0 %collective-permute-start.10 = (f32[30,1,256]{2,1,0:T(1,128)S(1)}, f32[30,1,256]{2,1,0:T(1,128)S(1)}, u32[]{:S(2)}, u32[]{:S(2)}) collective-permute-start(f32[30,1,256]{2,1,0:T(1,128)S(1)} %get-tuple-element.174), channel_id=1, source_target_pairs={{4,0},{8,4},{12,8},{5,1},{9,5},{13,9},{6,2},{10,6},{14,10},{7,3},{... | collective-permute-start | bytes 92168 | tf_op jit(solution)/shard_map/ppermute | solution.py:26
  140.7 3.9 %collective-permute-start.9 = (f32[30,1,256]{2,1,0:T(1,128)S(1)}, f32[30,1,256]{2,1,0:T(1,128)S(1)}, u32[]{:S(2)}, u32[]{:S(2)}) collective-permute-start(f32[30,1,256]{2,1,0:T(1,128)S(1)} %get-tuple-element.173), channel_id=1, source_target_pairs={{0,4},{4,8},{8,12},{1,5},{5,9},{9,13},{2,6},{6,10},{10,14},{3,7},{... | collective-permute-start | bytes 92168 | tf_op jit(solution)/shard_map/ppermute | solution.py:23
  147.4 7.2 %collective-permute-start.11 = (f32[30,34,1]{1,2,0:T(1,128)S(1)}, f32[30,34,1]{1,2,0:T(1,128)S(1)}, u32[]{:S(2)}, u32[]{:S(2)}) collective-permute-start(f32[30,34,1]{1,2,0:T(1,128)S(1)} %copy.141), channel_id=1, source_target_pairs={{0,1},{1,2},{2,3},{4,5},{5,6},{6,7},{8,9},{9,10},{10,11},{12,13},{... | collective-permute-start | bytes 12248 | tf_op jit(solution)/shard_map/ppermute | solution.py:23
  152.6 5.6 %collective-permute-start.12 = (f32[30,34,1]{1,2,0:T(1,128)S(1)}, f32[30,34,1]{1,2,0:T(1,128)S(1)}, u32[]{:S(2)}, u32[]{:S(2)}) collective-permute-start(f32[30,34,1]{1,2,0:T(1,128)S(1)} %copy.142), channel_id=1, source_target_pairs={{1,0},{2,1},{3,2},{5,4},{6,5},{7,6},{9,8},{10,9},{11,10},{13,12},{... | collective-permute-start | bytes 12248 | tf_op jit(solution)/shard_map/ppermute | solution.py:26
  204.3 27.3 %copy-start.4 = (f32[30,32,256]{2,1,0:T(8,128)}, f32[30,32,256]{2,1,0:T(8,128)S(1)}, u32[]{:S(2)}) copy-start(f32[30,32,256]{2,1,0:T(8,128)S(1)} %subtract_divide_fusion) | copy-start | bytes 2949124
  204.3 2.6 collective-permute-start.13
  205.6 7.4 %collective-permute-start.14 = (f32[30,1,256]{2,1,0:T(1,128)S(1)}, f32[30,1,256]{2,1,0:T(1,128)S(1)}, u32[]{:S(2)}, u32[]{:S(2)}) collective-permute-start(f32[30,1,256]{2,1,0:T(1,128)S(1)} %get-tuple-element.172), channel_id=1, source_target_pairs={{4,0},{8,4},{12,8},{5,1},{9,5},{13,9},{6,2},{10,6},{14,10},{7,3},{... | collective-permute-start | bytes 92168 | tf_op jit(solution)/shard_map/ppermute | solution.py:26
  215.8 13.4 %collective-permute-start.15 = (f32[30,34,1]{1,2,0:T(1,128)S(1)}, f32[30,34,1]{1,2,0:T(1,128)S(1)}, u32[]{:S(2)}, u32[]{:S(2)}) collective-permute-start(f32[30,34,1]{1,2,0:T(1,128)S(1)} %copy.147), channel_id=1, source_target_pairs={{0,1},{1,2},{2,3},{4,5},{5,6},{6,7},{8,9},{9,10},{10,11},{12,13},{... | collective-permute-start | bytes 12248 | tf_op jit(solution)/shard_map/ppermute | solution.py:23
  221.2 9.2 %collective-permute-start.16 = (f32[30,34,1]{1,2,0:T(1,128)S(1)}, f32[30,34,1]{1,2,0:T(1,128)S(1)}, u32[]{:S(2)}, u32[]{:S(2)}) collective-permute-start(f32[30,34,1]{1,2,0:T(1,128)S(1)} %copy.148), channel_id=1, source_target_pairs={{1,0},{2,1},{3,2},{5,4},{6,5},{7,6},{9,8},{10,9},{11,10},{13,12},{... | collective-permute-start | bytes 12248 | tf_op jit(solution)/shard_map/ppermute | solution.py:26
  234.0 51.3 %copy-start.3 = (f32[1,30,32,256]{3,2,1,0:T(8,128)S(1)}, f32[1,30,32,256]{3,2,1,0:T(8,128)}, u32[]{:S(2)}) copy-start(f32[1,30,32,256]{3,2,1,0:T(8,128)} %param.29) | copy-start | bytes 2949124
  (19 other events, 55.6 us)
where the time goes:
time: 291 us; the launch traced here: 290 us
  blocking collectives  129 us (44%)
  other arithmetic  53.6 us (18%)
  local copies, waits for them, and re-layouts  43 us (15%)
  starting transfers between devices  35 us (12%)
  waiting for transfers between devices  17.6 us (6%)
  between operations  9.11 us (3%)
  matrix products  2.96 us (1%)
    psum x3, blocking collectives, body(): lax.psum((partials, jnp.sum(interior_vector * interior_vector)), ('gx', '...  94.4 us
    psum x1, blocking collectives, body(): beta = jnp.sqrt(lax.psum(jnp.sum(rhs * rhs), ('gx', 'gy')))  34.1 us
    ppermute x8, starting transfers between devices, extended(): lax.ppermute(lax.slice_in_dim(block, block.shape[dim] - width, None, axis...  21.4 us
    ppermute x8, waiting for transfers between devices, extended(): lax.ppermute(lax.slice_in_dim(block, 0, width, axis=dim), axis, backward)  17.3 us
    concatenate x8, other arithmetic, extended(): block = jnp.concatenate([low, block, high], axis=dim)  11.1 us
    ppermute x8, starting transfers between devices, extended(): lax.ppermute(lax.slice_in_dim(block, 0, width, axis=dim), axis, backward)  10.5 us
    reduce_sum x2, other arithmetic, body(): jnp.sum(interior_vector * near[i])  9.97 us
    slice x7, local copies, waits for them, and re-layouts, extended(): lax.slice_in_dim(block, 0, width, axis=dim)  6.84 us
  transfers between devices with their start and end apart: 17, of which 7 were waited for; matrix products, arithmetic and copies ran while one was open for 12% of the time, Pallas kernels for 0%

commit v1 on v0

--- a/solution.py
+++ b/solution.py
@@ -122,7 +122,7 @@
         interior_vector = krylov_vector
         partials = jnp.stack([jnp.sum(interior_vector * near[i]) for i in range(j + 1)])
         heights, squared = lax.psum(
-            (partials, jnp.sum(interior_vector * interior_vector)), ("gx", "gy")
+            lax.psum((partials, jnp.sum(interior_vector * interior_vector)), "gy"), "gx"
         )
         for i in range(j + 1):
             krylov_vector = krylov_vector - heights[i] * near[i]

time: 291 us -> 246 us (0.85)
  blocking collectives: 129 us -> 86 us
    psum x3 -> x6, blocking collectives: 94.4 us -> 51.9 us  [the longest x3 30.1 us: body(): lax.psum((partials, jnp.sum(interior_vector * interior_vector)), 'gy')]
  transfers between devices with their start and end apart: 17 -> 17, of which waited for: 7 -> 7; matrix products, arithmetic and copies ran while one was open for 12% -> 14% of each run, Pallas kernels for 0% -> 0%
where the time goes in v1:
time: 246 us; the launch traced here: 245 us
  blocking collectives  86 us (35%)
  other arithmetic  53.8 us (22%)
  local copies, waits for them, and re-layouts  42.8 us (17%)
  starting transfers between devices  35.3 us (14%)
  waiting for transfers between devices  14.7 us (6%)
  between operations  9.2 us (4%)
  matrix products  2.95 us (1%)
    psum x1, blocking collectives, body(): beta = jnp.sqrt(lax.psum(jnp.sum(rhs * rhs), ('gx', 'gy')))  34.1 us
    psum x3, blocking collectives, body(): lax.psum((partials, jnp.sum(interior_vector * interior_vector)), 'gy')  30.1 us
    ppermute x8, starting transfers between devices, extended(): lax.ppermute(lax.slice_in_dim(block, block.shape[dim] - width, None, axis...  21.8 us
    psum x3, blocking collectives, body(): lax.psum(lax.psum((partials, jnp.sum(interior_vector * interior_vector)),...  21.7 us
    ppermute x8, waiting for transfers between devices, extended(): lax.ppermute(lax.slice_in_dim(block, 0, width, axis=dim), axis, backward)  14.6 us
    concatenate x8, other arithmetic, extended(): block = jnp.concatenate([low, block, high], axis=dim)  11.1 us
    ppermute x8, starting transfers between devices, extended(): lax.ppermute(lax.slice_in_dim(block, 0, width, axis=dim), axis, backward)  10.5 us
    reduce_sum x2, other arithmetic, body(): jnp.sum(interior_vector * near[i])  10 us
  transfers between devices with their start and end apart: 17, of which 7 were waited for; matrix products, arithmetic and copies ran while one was open for 14% of the time, Pallas kernels for 0%

profile of v1, /device:TPU:0, one launch (start us, length us, event | category | flops | bytes accessed | tf_op | source)
XLA Modules:
  0.0 244.8 jit_solution(15109669030849163453)
XLA Ops:
  2.5 3.1 %collective-permute-start = (f32[6,32,256]{2,0,1:T(8,128)}, f32[6,32,256]{2,0,1:T(8,128)}, u32[]{:S(2)}, u32[]{:S(2)}) collective-permute-start(f32[6,32,256]{2,0,1:T(8,128)} %bitcast.108), channel_id=1, source_target_pairs={{0,16},{16,0},{1,17},{17,1},{2,18},{18,2},{3,19},{19,3},{4,20},{20... | collective-permute-start | bytes 589832 | tf_op jit(solution)/shard_map/ppermute | solution.py:15
  17.1 4.1 %collective-permute-start.3 = (f32[2,30,34,1]{2,0,3,1:T(2,128)S(1)}, f32[2,30,34,1]{2,0,3,1:T(2,128)}, u32[]{:S(2)}, u32[]{:S(2)}) collective-permute-start(f32[2,30,34,1]{2,0,3,1:T(2,128)S(1)} %copy.131), channel_id=1, source_target_pairs={{0,1},{1,2},{2,3},{4,5},{5,6},{6,7},{8,9},{9,10},{10,11},{12,13},{... | collective-permute-start | bytes 24488 | tf_op jit(solution)/shard_map/ppermute | solution.py:23
  30.8 3.2 %pad_maximum_fusion = f32[2,30,34,258]{3,2,1,0:T(8,128)S(1)} fusion(f32[2,30,34,1]{3,2,1,0:T(8,128)} %copy.134, f32[2,30,1,256]{3,2,1,0:T(1,128)S(1)} %collective-permute-done.2, f32[1,30,32,256]{3,2,1,0:T(8,128)S(1)} %add_multiply_fusion, f32[1,30,32,256]{3,2,1,0:T(8,128)S(1)} %copy-done.2, f32[2,30,1,256]{3,2,1,0:T(1,128)S(1)} %collective-permute-done.1, ...), kind=kLoop, calls=%fused_computation.1 | loop fusion | flops 2631600 | bytes 4210560 | tf_op jit(solution)/shard_map/concatenate | solution.py:27
  39.7 5.6 %multiply_reduce_fusion.9 = (f32[]{:T(128)}, f32[30,32,256]{2,1,0:T(8,128)S(1)}, f32[30,32,256]{2,1,0:T(8,128)}, f32[30,32,256]{2,1,0:T(8,128)}, f32[30,32,256]{...) fusion(f32[30,32,256]{2,1,0:T(8,128)S(1)} %fusion.80, ...), kind=kLoop, calls=%fused_computation.156 | loop fusion | flops 7864319 | bytes 21381124 | tf_op jit(solution)/shard_map/reduce_sum | solution.py:113
  45.3 34.1 %psum.91 = f32[]{:T(128)} all-reduce(f32[]{:T(128)} %get-tuple-element.155), channel_id=1, replica_groups=mesh['comp'=2,'gx'=4,'gy'=4] {'gx','gy'}, use_global_device_ids=true, to_apply=%region_3.4 | all-reduce | flops 1 | bytes 8 | tf_op jit(solution)/shard_map/psum | solution.py:113
  82.9 4.0 %collective-permute-done.6 = f32[30,1,256]{2,1,0:T(1,128)S(1)} collective-permute-done((f32[30,1,256]{2,1,0:T(1,128)S(1)}, f32[30,1,256]{2,1,0:T(1,128)S(1)}, u32[]{:S(2)}, u32[]{:S(2)}) %collective-permute-start.6) | collective-permute-done | bytes 30752 | tf_op jit(solution)/shard_map/ppermute | solution.py:26
  87.6 2.4 collective-permute-start.7
  97.1 2.4 select_maximum_fusion.8
  99.6 5.1 %multiply_reduce_fusion.8 = (f32[]{:T(128)}, f32[]{:T(128)}, f32[30,32,256]{2,1,0:T(8,128)}) fusion(f32[30,32,256]{2,1,0:T(8,128)S(1)} %broadcast_divide_fusion, f32[30,32,256]{2,1,0:T(8,128)} %get-tuple-element.162, f32[30,1,256]{2,1,0:T(1,128)S(1)} %collective-permute-done.6, f32[30,1,256]{2,1,0:T(1,128)S(1)} %collective-permute-done.5, ...), kind=kLoop, calls=%fused_computation.155 | loop fusion | flops 7618558 | bytes 9900012 | tf_op jit(solution)/shard_map/reduce_sum | solution.py:123
  104.7 9.4 %all-reduce.9 = (f32[]{:T(128)}, f32[1]{0:T(128)}) all-reduce(f32[]{:T(128)} %get-tuple-element.140, f32[1]{0:T(128)} %bitcast.21), channel_id=1, replica_groups=mesh['comp'=2,'gx'=4,'gy'=4] {'gy'}, use_global_device_ids=true, to_apply=%region_8.9 | all-reduce | flops 2 | bytes 16 | tf_op jit(solution)/shard_map/psum | solution.py:125
  114.0 6.7 %all-reduce.12 = (f32[]{:T(128)}, f32[1]{0:T(128)}) all-reduce(f32[]{:T(128)} %get-tuple-element.145, f32[1]{0:T(128)} %get-tuple-element.146), channel_id=1, replica_groups=mesh['comp'=2,'gx'=4,'gy'=4] {'gx'}, use_global_device_ids=true, to_apply=%region_9.10 | all-reduce | flops 2 | bytes 16 | tf_op jit(solution)/shard_map/psum | solution.py:124
  126.1 3.0 %collective-permute-start.9 = (f32[30,1,256]{2,1,0:T(1,128)S(1)}, f32[30,1,256]{2,1,0:T(1,128)S(1)}, u32[]{:S(2)}, u32[]{:S(2)}) collective-permute-start(f32[30,1,256]{2,1,0:T(1,128)S(1)} %get-tuple-element.179), channel_id=1, source_target_pairs={{0,4},{4,8},{8,12},{1,5},{5,9},{9,13},{2,6},{6,10},{10,14},{3,7},{... | collective-permute-start | bytes 92168 | tf_op jit(solution)/shard_map/ppermute | solution.py:23
  132.7 3.6 %collective-permute-start.11 = (f32[30,34,1]{1,2,0:T(1,128)S(1)}, f32[30,34,1]{1,2,0:T(1,128)S(1)}, u32[]{:S(2)}, u32[]{:S(2)}) collective-permute-start(f32[30,34,1]{1,2,0:T(1,128)S(1)} %copy.141), channel_id=1, source_target_pairs={{0,1},{1,2},{2,3},{4,5},{5,6},{6,7},{8,9},{9,10},{10,11},{12,13},{... | collective-permute-start | bytes 12248 | tf_op jit(solution)/shard_map/ppermute | solution.py:23
  140.7 2.5 %collective-permute-done.12 = f32[30,34,1]{1,2,0:T(1,128)S(1)} collective-permute-done((f32[30,34,1]{1,2,0:T(1,128)S(1)}, f32[30,34,1]{1,2,0:T(1,128)S(1)}, u32[]{:S(2)}, u32[]{:S(2)}) %collective-permute-start.12) | collective-permute-done | bytes 4112 | tf_op jit(solution)/shard_map/ppermute | solution.py:26
  146.9 5.0 %multiply_reduce_fusion.6 = (f32[]{:T(128)}, f32[]{:T(128)}, f32[]{:T(128)}, f32[30,32,256]{2,1,0:T(8,128)}) fusion(f32[30,32,256]{2,1,0:T(8,128)S(1)} %subtract_divide_fusion.1, f32[30,32,256]{2,1,0:T(8,128)} %get-tuple-element.162, f32[30,1,256]{2,1,0:T(1,128)S(1)} %collective-permute-done.10, f32[30,1,256]{2,1,0:T(1,128)S(1)} %collective-permute-done.9, ...), kind=kLoop, calls=%fused_computation.152 | loop fusion | flops 8355837 | bytes 10883060 | tf_op jit(solution)/shard_map/reduce_sum | solution.py:123
  153.1 9.1 %all-reduce.8 = (f32[]{:T(128)}, f32[2]{0:T(128)S(1)}) all-reduce(f32[]{:T(128)} %get-tuple-element.137, f32[2]{0:T(128)S(1)} %pad_maximum_fusion.31), channel_id=1, replica_groups=mesh['comp'=2,'gx'=4,'gy'=4] {'gy'}, use_global_device_ids=true, to_apply=%region_15.16 | all-reduce | flops 3 | bytes 24 | tf_op jit(solution)/shard_map/psum | solution.py:125
  162.2 8.3 %all-reduce.11 = (f32[]{:T(128)}, f32[2]{0:T(128)S(1)}) all-reduce(f32[]{:T(128)} %get-tuple-element.143, f32[2]{0:T(128)S(1)} %get-tuple-element.144), channel_id=1, replica_groups=mesh['comp'=2,'gx'=4,'gy'=4] {'gx'}, use_global_device_ids=true, to_apply=%region_16.17 | all-reduce | flops 3 | bytes 24 | tf_op jit(solution)/shard_map/psum | solution.py:124
  173.3 2.8 %subtract_divide_fusion = f32[30,32,256]{2,1,0:T(8,128)S(1)} fusion(f32[30,32,256]{2,1,0:T(8,128)S(1)} %subtract_divide_fusion.1, f32[30,32,256]{2,1,0:T(8,128)} %get-tuple-element.153, f32[]{:T(128)} %sqrt.14, f32[]{:T(128)} %bitcast.35, f32[]{:T(128)} %bitcast.34, f32[30,32,256]{2,1,0:T(8,128)S(1)} %get-tuple-element.156, f32[]{:T(128)S(6)} %sqrt.12), kind=kLoop, calls=%fused_computation.149 | loop fusion | flops 1474560 | bytes 3932176 | tf_op jit(solution)/shard_map/div | solution.py:133
  179.7 3.3 %collective-permute-done.14 = f32[30,1,256]{2,1,0:T(1,128)S(1)} collective-permute-done((f32[30,1,256]{2,1,0:T(1,128)S(1)}, f32[30,1,256]{2,1,0:T(1,128)S(1)}, u32[]{:S(2)}, u32[]{:S(2)}) %collective-permute-start.14) | collective-permute-done | bytes 30752 | tf_op jit(solution)/shard_map/ppermute | solution.py:26
  185.7 3.7 %collective-permute-start.15 = (f32[30,34,1]{1,2,0:T(1,128)S(1)}, f32[30,34,1]{1,2,0:T(1,128)S(1)}, u32[]{:S(2)}, u32[]{:S(2)}) collective-permute-start(f32[30,34,1]{1,2,0:T(1,128)S(1)} %copy.147), channel_id=1, source_target_pairs={{0,1},{1,2},{2,3},{4,5},{5,6},{6,7},{8,9},{9,10},{10,11},{12,13},{... | collective-permute-start | bytes 12248 | tf_op jit(solution)/shard_map/ppermute | solution.py:23
  203.6 6.0 %multiply_reduce_fusion = (f32[]{:T(128)}, f32[]{:T(128)}, f32[]{:T(128)}, f32[]{:T(128)}) fusion(f32[30,32,256]{2,1,0:T(8,128)} %copy-done.4, f32[30,32,256]{2,1,0:T(8,128)S(1)} %subtract_divide_fusion.1, f32[30,32,256]{2,1,0:T(8,128)} %get-tuple-element.162, f32[30,1,256]{2,1,0:T(1,128)S(1)} %collective-permute-done.14, ...), kind=kLoop, calls=%fused_computation.145 | loop fusion | flops 8847356 | bytes 10883064 | tf_op jit(solution)/shard_map/reduce_sum | solution.py:125
  211.5 11.7 %all-reduce.7 = (f32[3]{0:T(128)S(1)}, f32[]{:T(128)}) all-reduce(f32[3]{0:T(128)S(1)} %pad_maximum_fusion.32, f32[]{:T(128)} %get-tuple-element.132), channel_id=1, replica_groups=mesh['comp'=2,'gx'=4,'gy'=4] {'gy'}, use_global_device_ids=true, to_apply=%region_22.23 | all-reduce | flops 4 | bytes 32 | tf_op jit(solution)/shard_map/psum | solution.py:125
  223.2 6.7 %all-reduce.10 = (f32[3]{0:T(128)S(1)}, f32[]{:T(128)}) all-reduce(f32[3]{0:T(128)S(1)} %get-tuple-element.141, f32[]{:T(128)} %get-tuple-element.142), channel_id=1, replica_groups=mesh['comp'=2,'gx'=4,'gy'=4] {'gx'}, use_global_device_ids=true, to_apply=%region_23.24 | all-reduce | flops 4 | bytes 32 | tf_op jit(solution)/shard_map/psum | solution.py:124
  240.4 4.4 %fusion.74 = f32[1,30,32,256]{3,2,1,0:T(8,128)} fusion(f32[1,30,32,256]{3,2,1,0:T(8,128)S(1)} %copy-done.3, f32[30,32,256]{2,1,0:T(8,128)} %copy-done.4, f32[30,32,256]{2,1,0:T(8,128)S(1)} %subtract_divide_fusion.1, f32[]{:T(128)} %bitcast.55, f32[]{:T(128)} %bitcast.54, f32[]{:T(128)} %bitcast.53, f32[30,32,256]{2,1,0:T(8,128)S(1)} %get-tuple-element.156, ...), kind=kLoop, calls=%fused_computation.144 | loop fusion | flops 1720320 | bytes 4915216 | tf_op jit(solution)/shard_map/broadcast_in_dim | solution.py:139
  (166 shorter events, 85.5 us)
Async XLA Ops:
  0.6 36.8 %copy-start = (f32[1,256,128]{2,1,0:T(8,128)S(1)}, f32[1,256,128]{2,1,0:T(8,128)}, u32[]{:S(2)}) copy-start(f32[1,256,128]{2,1,0:T(8,128)} %param.37) | copy-start | bytes 393220
  2.5 7.6 %copy-start.24 = (s32[1,32]{1,0:T(1,128)S(1)}, s32[1,32]{1,0:T(1,128)}, u32[]{:S(2)}) copy-start(s32[1,32]{1,0:T(1,128)} %param.36) | copy-start | bytes 388
  2.5 8.2 %copy-start.18 = (s32[1,32,256]{2,1,0:T(8,128)S(1)}, s32[1,32,256]{2,1,0:T(8,128)}, u32[]{:S(2)}) copy-start(s32[1,32,256]{2,1,0:T(8,128)} %param.33) | copy-start | bytes 98308
  2.5 8.2 %copy-start.23 = (f32[16,2]{0,1:T(2,128)S(1)}, f32[16,2]{0,1:T(2,128)}, u32[]{:S(2)}) copy-start(f32[16,2]{0,1:T(2,128)} %param.34) | copy-start | bytes 388
  2.5 32.9 %collective-permute-start = (f32[6,32,256]{2,0,1:T(8,128)}, f32[6,32,256]{2,0,1:T(8,128)}, u32[]{:S(2)}, u32[]{:S(2)}) collective-permute-start(f32[6,32,256]{2,0,1:T(8,128)} %bitcast.108), channel_id=1, source_target_pairs={{0,16},{16,0},{1,17},{17,1},{2,18},{18,2},{3,19},{19,3},{4,20},{20... | collective-permute-start | bytes 589832 | tf_op jit(solution)/shard_map/ppermute | solution.py:15
  7.4 6.0 %collective-permute-start.1 = (f32[2,30,1,256]{3,2,1,0:T(1,128)S(1)}, f32[2,30,1,256]{3,2,1,0:T(1,128)S(1)}, u32[]{:S(2)}, u32[]{:S(2)}) collective-permute-start(f32[2,30,1,256]{3,2,1,0:T(1,128)S(1)} %get-tuple-element.169), channel_id=1, source_target_pairs={{0,4},{4,8},{8,12},{1,5},{5,9},{9,13},{2,6},{6,10},{10,14},{3,7},{... | collective-permute-start | bytes 184328 | tf_op jit(solution)/shard_map/ppermute | solution.py:23
  8.8 4.7 %collective-permute-start.2 = (f32[2,30,1,256]{3,2,1,0:T(1,128)S(1)}, f32[2,30,1,256]{3,2,1,0:T(1,128)S(1)}, u32[]{:S(2)}, u32[]{:S(2)}) collective-permute-start(f32[2,30,1,256]{3,2,1,0:T(1,128)S(1)} %get-tuple-element.170), channel_id=1, source_target_pairs={{4,0},{8,4},{12,8},{5,1},{9,5},{13,9},{6,2},{10,6},{14,10},{7,3},{... | collective-permute-start | bytes 184328 | tf_op jit(solution)/shard_map/ppermute | solution.py:26
  17.1 7.8 %collective-permute-start.3 = (f32[2,30,34,1]{2,0,3,1:T(2,128)S(1)}, f32[2,30,34,1]{2,0,3,1:T(2,128)}, u32[]{:S(2)}, u32[]{:S(2)}) collective-permute-start(f32[2,30,34,1]{2,0,3,1:T(2,128)S(1)} %copy.131), channel_id=1, source_target_pairs={{0,1},{1,2},{2,3},{4,5},{5,6},{6,7},{8,9},{9,10},{10,11},{12,13},{... | collective-permute-start | bytes 24488 | tf_op jit(solution)/shard_map/ppermute | solution.py:23
  22.4 6.1 %collective-permute-start.4 = (f32[2,30,34,1]{2,0,3,1:T(2,128)}, f32[2,30,34,1]{2,0,3,1:T(2,128)}, u32[]{:S(2)}, u32[]{:S(2)}) collective-permute-start(f32[2,30,34,1]{2,0,3,1:T(2,128)} %copy.132), channel_id=1, source_target_pairs={{1,0},{2,1},{3,2},{5,4},{6,5},{7,6},{9,8},{10,9},{11,10},{13,12},{... | collective-permute-start | bytes 24488 | tf_op jit(solution)/shard_map/ppermute | solution.py:26
  80.3 2.6 %collective-permute-start.5 = (f32[30,1,256]{2,1,0:T(1,128)S(1)}, f32[30,1,256]{2,1,0:T(1,128)S(1)}, u32[]{:S(2)}, u32[]{:S(2)}) collective-permute-start(f32[30,1,256]{2,1,0:T(1,128)S(1)} %get-tuple-element.181), channel_id=1, source_target_pairs={{0,4},{4,8},{8,12},{1,5},{5,9},{9,13},{2,6},{6,10},{10,14},{3,7},{... | collective-permute-start | bytes 92168 | tf_op jit(solution)/shard_map/ppermute | solution.py:23
  81.6 5.3 %collective-permute-start.6 = (f32[30,1,256]{2,1,0:T(1,128)S(1)}, f32[30,1,256]{2,1,0:T(1,128)S(1)}, u32[]{:S(2)}, u32[]{:S(2)}) collective-permute-start(f32[30,1,256]{2,1,0:T(1,128)S(1)} %get-tuple-element.182), channel_id=1, source_target_pairs={{4,0},{8,4},{12,8},{5,1},{9,5},{13,9},{6,2},{10,6},{14,10},{7,3},{... | collective-permute-start | bytes 92168 | tf_op jit(solution)/shard_map/ppermute | solution.py:26
  87.6 4.8 %collective-permute-start.7 = (f32[30,34,1]{1,2,0:T(1,128)S(1)}, f32[30,34,1]{1,2,0:T(1,128)S(1)}, u32[]{:S(2)}, u32[]{:S(2)}) collective-permute-start(f32[30,34,1]{1,2,0:T(1,128)S(1)} %copy.135), channel_id=1, source_target_pairs={{0,1},{1,2},{2,3},{4,5},{5,6},{6,7},{8,9},{9,10},{10,11},{12,13},{... | collective-permute-start | bytes 12248 | tf_op jit(solution)/shard_map/ppermute | solution.py:23
  90.3 5.6 %collective-permute-start.8 = (f32[30,34,1]{1,2,0:T(1,128)S(1)}, f32[30,34,1]{1,2,0:T(1,128)S(1)}, u32[]{:S(2)}, u32[]{:S(2)}) collective-permute-start(f32[30,34,1]{1,2,0:T(1,128)S(1)} %copy.136), channel_id=1, source_target_pairs={{1,0},{2,1},{3,2},{5,4},{6,5},{7,6},{9,8},{10,9},{11,10},{13,12},{... | collective-permute-start | bytes 12248 | tf_op jit(solution)/shard_map/ppermute | solution.py:26
  104.7 24.5 %copy-start.25 = (s32[2]{0:T(128)S(1)}, s32[2]{0:T(128)}, u32[]{:S(2)}) copy-start(s32[2]{0:T(128)} %constant.341.clone.1) | copy-start | bytes 28
  124.8 5.1 %collective-permute-start.10 = (f32[30,1,256]{2,1,0:T(1,128)S(1)}, f32[30,1,256]{2,1,0:T(1,128)S(1)}, u32[]{:S(2)}, u32[]{:S(2)}) collective-permute-start(f32[30,1,256]{2,1,0:T(1,128)S(1)} %get-tuple-element.180), channel_id=1, source_target_pairs={{4,0},{8,4},{12,8},{5,1},{9,5},{13,9},{6,2},{10,6},{14,10},{7,3},{... | collective-permute-start | bytes 92168 | tf_op jit(solution)/shard_map/ppermute | solution.py:26
  126.1 3.9 %collective-permute-start.9 = (f32[30,1,256]{2,1,0:T(1,128)S(1)}, f32[30,1,256]{2,1,0:T(1,128)S(1)}, u32[]{:S(2)}, u32[]{:S(2)}) collective-permute-start(f32[30,1,256]{2,1,0:T(1,128)S(1)} %get-tuple-element.179), channel_id=1, source_target_pairs={{0,4},{4,8},{8,12},{1,5},{5,9},{9,13},{2,6},{6,10},{10,14},{3,7},{... | collective-permute-start | bytes 92168 | tf_op jit(solution)/shard_map/ppermute | solution.py:23
  132.7 6.9 %collective-permute-start.11 = (f32[30,34,1]{1,2,0:T(1,128)S(1)}, f32[30,34,1]{1,2,0:T(1,128)S(1)}, u32[]{:S(2)}, u32[]{:S(2)}) collective-permute-start(f32[30,34,1]{1,2,0:T(1,128)S(1)} %copy.141), channel_id=1, source_target_pairs={{0,1},{1,2},{2,3},{4,5},{5,6},{6,7},{8,9},{9,10},{10,11},{12,13},{... | collective-permute-start | bytes 12248 | tf_op jit(solution)/shard_map/ppermute | solution.py:23
  137.7 5.6 %collective-permute-start.12 = (f32[30,34,1]{1,2,0:T(1,128)S(1)}, f32[30,34,1]{1,2,0:T(1,128)S(1)}, u32[]{:S(2)}, u32[]{:S(2)}) collective-permute-start(f32[30,34,1]{1,2,0:T(1,128)S(1)} %copy.142), channel_id=1, source_target_pairs={{1,0},{2,1},{3,2},{5,4},{6,5},{7,6},{9,8},{10,9},{11,10},{13,12},{... | collective-permute-start | bytes 12248 | tf_op jit(solution)/shard_map/ppermute | solution.py:26
  176.1 25.0 %copy-start.4 = (f32[30,32,256]{2,1,0:T(8,128)}, f32[30,32,256]{2,1,0:T(8,128)S(1)}, u32[]{:S(2)}) copy-start(f32[30,32,256]{2,1,0:T(8,128)S(1)} %subtract_divide_fusion) | copy-start | bytes 2949124
  176.1 3.6 %collective-permute-start.13 = (f32[30,1,256]{2,1,0:T(1,128)S(1)}, f32[30,1,256]{2,1,0:T(1,128)S(1)}, u32[]{:S(2)}, u32[]{:S(2)}) collective-permute-start(f32[30,1,256]{2,1,0:T(1,128)S(1)} %get-tuple-element.177), channel_id=1, source_target_pairs={{0,4},{4,8},{8,12},{1,5},{5,9},{9,13},{2,6},{6,10},{10,14},{3,7},{... | collective-permute-start | bytes 92168 | tf_op jit(solution)/shard_map/ppermute | solution.py:23
  178.4 4.6 %collective-permute-start.14 = (f32[30,1,256]{2,1,0:T(1,128)S(1)}, f32[30,1,256]{2,1,0:T(1,128)S(1)}, u32[]{:S(2)}, u32[]{:S(2)}) collective-permute-start(f32[30,1,256]{2,1,0:T(1,128)S(1)} %get-tuple-element.178), channel_id=1, source_target_pairs={{4,0},{8,4},{12,8},{5,1},{9,5},{13,9},{6,2},{10,6},{14,10},{7,3},{... | collective-permute-start | bytes 92168 | tf_op jit(solution)/shard_map/ppermute | solution.py:26
  185.7 13.1 %collective-permute-start.15 = (f32[30,34,1]{1,2,0:T(1,128)S(1)}, f32[30,34,1]{1,2,0:T(1,128)S(1)}, u32[]{:S(2)}, u32[]{:S(2)}) collective-permute-start(f32[30,34,1]{1,2,0:T(1,128)S(1)} %copy.147), channel_id=1, source_target_pairs={{0,1},{1,2},{2,3},{4,5},{5,6},{6,7},{8,9},{9,10},{10,11},{12,13},{... | collective-permute-start | bytes 12248 | tf_op jit(solution)/shard_map/ppermute | solution.py:23
  190.8 9.1 %collective-permute-start.16 = (f32[30,34,1]{1,2,0:T(1,128)S(1)}, f32[30,34,1]{1,2,0:T(1,128)S(1)}, u32[]{:S(2)}, u32[]{:S(2)}) collective-permute-start(f32[30,34,1]{1,2,0:T(1,128)S(1)} %copy.148), channel_id=1, source_target_pairs={{1,0},{2,1},{3,2},{5,4},{6,5},{7,6},{9,8},{10,9},{11,10},{13,12},{... | collective-permute-start | bytes 12248 | tf_op jit(solution)/shard_map/ppermute | solution.py:26
  203.6 36.8 %copy-start.3 = (f32[1,30,32,256]{3,2,1,0:T(8,128)S(1)}, f32[1,30,32,256]{3,2,1,0:T(8,128)}, u32[]{:S(2)}) copy-start(f32[1,30,32,256]{3,2,1,0:T(8,128)} %param.29) | copy-start | bytes 2949124
  (19 other events, 55.6 us)
